TPU v7x, 32 devices: a whole 2x2x4 slice. The times are simulated.
32 devices in a mesh: ctx: 8 (over y, x, core), tp: 4 (over z).
Axes of the slice: x: 2, y: 2, z: 4, core: 2. Of those that a mesh axis runs over, the one named last changes fastest.
Arguments:
- tokens: bfloat16 [4096, 4096], P('ctx', 'tp'), may hold values from -6 to 6
- norm_gain: float32 [4096], replicated, may hold values from 0.5 to 1.5
- proj_weight: bfloat16 [3, 4096, 2048], P(None, None, 'tp'), may hold values from -0.09375 to 0.09375
- short_taps: float32 [3, 3, 2048], P(None, None, 'tp'), may hold values from -1 to 1
- long_filter: float32 [4096, 2048], P('ctx', 'tp'), may hold values from -0.09375 to 0.09375
- skip_gain: float32 [2048], P('tp'), may hold values from -1 to 1
Outputs:
- output: bfloat16 [4096, 2048], P('ctx', 'tp')
All inputs are finite; a program needn't handle non-finite values.
Results may differ from a plain program's by a relative error of at most 0.0081.
Values may be sent and summed in bfloat16 or wider, within the bound.
A program may use at most 128 MiB of HBM per device.

v0:
```python
import math
import jax
import jax.numpy as jnp
from jax import lax
from jax.sharding import PartitionSpec as P

highest = lax.Precision.HIGHEST


def from_behind(array, axis, by):
    devices = lax.axis_size(axis)
    pairs = [(i, i + by) for i in range(devices) if 0 <= i + by < devices]
    return lax.ppermute(array, axis, pairs)


def outer_tables(part_count):
    frequency = jnp.arange(2 * part_count, dtype=jnp.int32)
    source = jnp.arange(part_count, dtype=jnp.int32)
    turn_count = frequency[:, None] * source[None, :] % (2 * part_count)
    angles = turn_count.astype(jnp.float32) * (math.pi / part_count)
    return (jnp.cos(angles), jnp.sin(angles))


def inner_tables(row_count):
    step_index = jnp.arange(row_count, dtype=jnp.int32)
    turn_count = step_index[:, None] * step_index[None, :] % row_count
    angles = turn_count.astype(jnp.float32) * (2.0 * math.pi / row_count)
    return (jnp.cos(angles), jnp.sin(angles))


def twist_tables(own_index, part_count, block_rows, total_length):
    frequency = jnp.arange(2 * part_count, dtype=jnp.int32)
    column = own_index * block_rows + jnp.arange(block_rows, dtype=jnp.int32)
    turn_count = frequency[:, None] * column[None, :] % total_length
    angles = turn_count.astype(jnp.float32) * (2.0 * math.pi / total_length)
    return (jnp.cos(angles)[:, :, None], jnp.sin(angles)[:, :, None])


def forward_transform(signal, part_count, tables, regroup, spread):
    outer_cos, outer_sin, inner_cos, inner_sin, twist_cos, twist_sin = tables
    row_count, width_all = signal.shape
    block_rows = row_count // part_count
    regrouped = regroup(signal).reshape(part_count, block_rows, width_all)
    outer_real = jnp.einsum("an,njw->ajw", outer_cos, regrouped, precision=highest)
    outer_imag = -jnp.einsum("an,njw->ajw", outer_sin, regrouped, precision=highest)
    turned_real = outer_real * twist_cos + outer_imag * twist_sin
    turned_imag = outer_imag * twist_cos - outer_real * twist_sin
    arrived = spread(jnp.stack([turned_real, turned_imag]))
    spec_real = jnp.einsum("bj,ejw->ebw", inner_cos, arrived[0], precision=highest) + jnp.einsum(
        "bj,ejw->ebw", inner_sin, arrived[1], precision=highest
    )
    spec_imag = jnp.einsum("bj,ejw->ebw", inner_cos, arrived[1], precision=highest) - jnp.einsum(
        "bj,ejw->ebw", inner_sin, arrived[0], precision=highest
    )
    return (spec_real, spec_imag)


def inverse_transform(spec_real, spec_imag, part_count, tables):
    outer_cos, outer_sin, inner_cos, inner_sin, twist_cos, twist_sin = tables
    row_count = spec_real.shape[1]
    width_all = spec_real.shape[2]
    back_real = jnp.einsum("jb,ebw->ejw", inner_cos, spec_real, precision=highest) - jnp.einsum(
        "jb,ebw->ejw", inner_sin, spec_imag, precision=highest
    )
    back_imag = jnp.einsum("jb,ebw->ejw", inner_sin, spec_real, precision=highest) + jnp.einsum(
        "jb,ebw->ejw", inner_cos, spec_imag, precision=highest
    )
    arrived = lax.all_to_all(
        jnp.stack([back_real, back_imag]), "ctx", split_axis=2, concat_axis=1, tiled=True
    )
    turned_real = arrived[0] * twist_cos - arrived[1] * twist_sin
    turned_imag = arrived[0] * twist_sin + arrived[1] * twist_cos
    total_length = 2 * row_count * part_count
    folded = (
        jnp.einsum("an,ajw->njw", outer_cos, turned_real, precision=highest)
        - jnp.einsum("an,ajw->njw", outer_sin, turned_imag, precision=highest)
    ) / total_length
    return lax.all_to_all(
        folded.reshape(row_count, width_all), "ctx", split_axis=0, concat_axis=0, tiled=True
    )


def body(tokens, norm_gain, proj_weight, short_taps, long_filter, skip_gain):
    gathered = lax.all_gather(tokens, "tp", axis=1, tiled=True)
    widened = gathered.astype(jnp.float32)
    scaling = lax.rsqrt(jnp.mean(widened * widened, axis=1, keepdims=True) + 1e-06)
    normed = (widened * scaling * norm_gain).astype(jnp.bfloat16)
    projected = jnp.einsum(
        "td,bdc->btc", normed, proj_weight, preferred_element_type=jnp.float32
    ).astype(jnp.bfloat16)
    previous = from_behind(projected[:, -2:, :], "ctx", 1)
    extended = jnp.concatenate([previous, projected], axis=1).astype(jnp.float32)
    branch = (
        short_taps[:, 0, None, :] * extended[:, 2:, :]
        + short_taps[:, 1, None, :] * extended[:, 1:-1, :]
        + short_taps[:, 2, None, :] * extended[:, :-2, :]
    )
    mixed_field = branch[1] * branch[2]
    row_count, channels = mixed_field.shape
    part_count = lax.axis_size("ctx")
    own_index = lax.axis_index("ctx")
    block_rows = row_count // part_count
    total_length = 2 * row_count * part_count
    outer_cos, outer_sin = outer_tables(part_count)
    inner_cos, inner_sin = inner_tables(row_count)
    twist_cos, twist_sin = twist_tables(own_index, part_count, block_rows, total_length)
    tables = (outer_cos, outer_sin, inner_cos, inner_sin, twist_cos, twist_sin)
    gain_real, gain_imag = forward_transform(
        long_filter,
        part_count,
        tables,
        lambda values: lax.all_to_all(values, "ctx", split_axis=0, concat_axis=0, tiled=True),
        lambda values: lax.all_to_all(
            values.astype(jnp.bfloat16), "ctx", split_axis=1, concat_axis=2, tiled=True
        ).astype(values.dtype),
    )
    data_real, data_imag = forward_transform(
        mixed_field,
        part_count,
        tables,
        lambda values: lax.all_to_all(values, "ctx", split_axis=0, concat_axis=0, tiled=True),
        lambda values: lax.all_to_all(
            values.astype(jnp.bfloat16), "ctx", split_axis=1, concat_axis=2, tiled=True
        ).astype(values.dtype),
    )
    product_real = data_real * gain_real - data_imag * gain_imag
    product_imag = data_real * gain_imag + data_imag * gain_real
    convolved = inverse_transform(product_real, product_imag, part_count, tables)
    return (branch[0] * (convolved + skip_gain * mixed_field)).astype(jnp.bfloat16)


def solution(mesh):
    placed = (
        P("ctx", "tp"),
        P(),
        P(None, None, "tp"),
        P(None, None, "tp"),
        P("ctx", "tp"),
        P("tp"),
    )
    return jax.shard_map(
        body, mesh=mesh, in_specs=placed, out_specs=P("ctx", "tp"), check_vma=False
    )
```

profile of v0, /device:TPU:0, one launch (start us, length us, event | category | flops | bytes accessed | tf_op | source)
XLA Modules:
  0.0 390.0 jit_solution(1918648023505237398)
XLA Ops:
  7.3 5.2 %all-to-all-start.2 = ((f32[8,64,512]{2,1,0:T(8,128)}), f32[8,64,512]{2,1,0:T(8,128)}, u32[]{:S(2)}, u32[]{:S(2)}) async-start(f32[8,64,512]{2,1,0:T(8,128)} %bitcast.138), calls=%async_computation.2 | async-start | bytes 2097152 | tf_op jit(solution)/shard_map/all_to_all | solution.py:112
  12.5 79.9 %all-gather.2.cloned.1.call-done = bf16[512,4096]{1,0:T(8,128)(2,1)} async-done(((bf16[512,1024]{1,0:T(8,128)(2,1)}), bf16[512,4096]{1,0:T(8,128)(2,1)}) %all-gather.2.cloned.1.call-update) | async-done | bytes 4194320 | tf_op jit(solution)/shard_map/all_gather | solution.py:84
  95.9 9.9 %fusion.33 = bf16[3,512,512]{2,1,0:T(8,128)(2,1)S(1)} fusion(bf16[3,4096,512]{2,1,0:T(8,128)(2,1)} %param.8, bf16[512,4096]{1,0:T(8,128)(2,1)S(1)} %copy-done.3, f32[4096]{0:T(1024)S(1)} %copy-done.8, f32[512]{0:T(512)S(1)} %add_rsqrt_fusion), kind=kOutput, calls=%fused_computation.50 | convolution fusion | flops 6451625984 | bytes 18368512 | tf_op jit(solution)/shard_map/td,bdc->btc/dot_general | solution.py:88
  110.9 6.6 %all-to-all-start = ((f32[8,64,512]{2,1,0:T(8,128)}), f32[8,64,512]{2,1,0:T(8,128)}, u32[]{:S(2)}, u32[]{:S(2)}) async-start(f32[8,64,512]{2,1,0:T(8,128)} %bitcast.135), calls=%async_computation | async-start | bytes 2097152 | tf_op jit(solution)/shard_map/all_to_all | solution.py:121
  117.7 4.7 %fusion.75 = f32[16,64,512]{2,0,1:T(8,128)} fusion(f32[8,64,512]{2,1,0:T(8,128)} %all-to-all-done.2), kind=kOutput, calls=%fused_computation.89 | convolution fusion | flops 50333440 | bytes 3145728 | tf_op jit(solution)/shard_map/an,njw->ajw/dot_general | solution.py:45
  122.5 4.8 %fusion.77 = f32[16,64,512]{2,0,1:T(8,128)} fusion(f32[8,64,512]{2,1,0:T(8,128)} %all-to-all-done.2), kind=kOutput, calls=%fused_computation.91 | convolution fusion | flops 50333440 | bytes 3145728 | tf_op jit(solution)/shard_map/an,njw->ajw/dot_general | solution.py:44
  127.2 5.7 %all-to-all-done = f32[8,64,512]{2,1,0:T(8,128)} async-done(((f32[8,64,512]{2,1,0:T(8,128)}), f32[8,64,512]{2,1,0:T(8,128)}, u32[]{:S(2)}, u32[]{:S(2)}) %all-to-all-start) | async-done | bytes 1048608 | tf_op jit(solution)/shard_map/all_to_all | solution.py:121
  136.5 5.9 %fusion.47 = (bf16[1,16,64,512]{3,1,2,0:T(8,128)(2,1)S(1)}, bf16[1,16,64,512]{3,1,2,0:T(8,128)(2,1)S(1)}, bf16[1,16,64,512]{3,1,2,0:T(8,128)(2,1)}, bf16[1,16,64,512]{3,1,2,0:T(8,128)(2,1)}) fusion(f32[16,64,512]{2,0,1:T(8,128)S(1)} %copy-done.2, f32[16,64,512]{2,0,1:T(8,128)} %fusion.77, f32[16,64]{0,1:T(8,128)S(1)} %get-tuple-element.23, ...), kind=kOutput, calls=%fused_computation.58 | convolution fusion | flops 59770624 | bytes 11542528 | tf_op jit(solution)/shard_map/an,njw->ajw/dot_general | solution.py:44
  153.7 22.4 %all-to-all-done.3 = bf16[2,16,64,512]{3,2,0,1:T(8,128)(2,1)} async-done(((bf16[2,16,64,512]{3,2,0,1:T(8,128)(2,1)}), bf16[2,16,64,512]{3,2,0,1:T(8,128)(2,1)}, u32[]{:S(2)}, u32[]{:S(2)}) %all-to-all-start.3) | async-done | bytes 2097184 | tf_op jit(solution)/shard_map/all_to_all | solution.py:113
  182.9 6.9 %fusion.64 = f32[2,512,512]{2,1,0:T(8,128)S(1)} fusion(bf16[2,512,512]{2,1,0:T(8,128)(2,1)S(1)} %bitcast.141), kind=kOutput, calls=%fused_computation.78 | convolution fusion | flops 3224895488 | bytes 3145728 | tf_op jit(solution)/shard_map/bj,ejw->ebw/dot_general | solution.py:49
  189.8 6.9 %fusion.60 = f32[2,512,512]{2,1,0:T(8,128)S(1)} fusion(bf16[2,512,512]{2,1,0:T(8,128)(2,1)S(1)} %bitcast.139), kind=kOutput, calls=%fused_computation.74 | convolution fusion | flops 3224895488 | bytes 3145728 | tf_op jit(solution)/shard_map/bj,ejw->ebw/dot_general | solution.py:52
  196.8 7.4 %convolution_add_fusion = f32[2,512,512]{2,1,0:T(8,128)} fusion(f32[2,512,512]{2,1,0:T(8,128)S(1)} %fusion.64, bf16[2,512,512]{2,1,0:T(8,128)(2,1)S(1)} %bitcast.140), kind=kOutput, calls=%fused_computation.44 | convolution fusion | flops 3225419776 | bytes 5242880 | tf_op jit(solution)/shard_map/bj,ejw->ebw/dot_general | solution.py:49
  204.2 7.6 %convolution_subtract_fusion = f32[2,512,512]{2,1,0:T(8,128)} fusion(f32[2,512,512]{2,1,0:T(8,128)S(1)} %fusion.60, bf16[2,512,512]{2,1,0:T(8,128)(2,1)S(1)} %bitcast.142), kind=kOutput, calls=%fused_computation.42 | convolution fusion | flops 3225419776 | bytes 5242880 | tf_op jit(solution)/shard_map/bj,ejw->ebw/dot_general | solution.py:52
  214.0 6.9 %fusion.62 = f32[2,512,512]{2,1,0:T(8,128)S(1)} fusion(bf16[2,512,512]{2,1,0:T(8,128)(2,1)S(1)} %bitcast.143), kind=kOutput, calls=%fused_computation.76 | convolution fusion | flops 3224895488 | bytes 3145728 | tf_op jit(solution)/shard_map/bj,ejw->ebw/dot_general | solution.py:52
  220.9 6.9 %fusion.66 = f32[2,512,512]{2,1,0:T(8,128)S(1)} fusion(bf16[2,512,512]{2,1,0:T(8,128)(2,1)S(1)} %bitcast.136), kind=kOutput, calls=%fused_computation.80 | convolution fusion | flops 3224895488 | bytes 3145728 | tf_op jit(solution)/shard_map/bj,ejw->ebw/dot_general | solution.py:49
  227.9 7.4 %convolution_add_fusion.1 = f32[2,512,512]{2,1,0:T(8,128)S(1)} fusion(f32[2,512,512]{2,1,0:T(8,128)S(1)} %fusion.66, bf16[2,512,512]{2,1,0:T(8,128)(2,1)S(1)} %bitcast.144), kind=kOutput, calls=%fused_computation.45 | convolution fusion | flops 3225419776 | bytes 5242880 | tf_op jit(solution)/shard_map/bj,ejw->ebw/dot_general | solution.py:49
  235.3 7.5 %multiply_subtract_fusion = (f32[2,512,512]{2,1,0:T(8,128)S(1)}, f32[2,512,512]{2,1,0:T(8,128)S(1)}) fusion(f32[2,512,512]{2,1,0:T(8,128)S(1)} %copy-done.5, f32[2,512,512]{2,1,0:T(8,128)S(1)} %convolution_add_fusion.1, f32[2,512,512]{2,1,0:T(8,128)S(1)} %copy-done.4, f32[2,512,512]{2,1,0:T(8,128)S(1)} %fusion.62, bf16[2,512,512]{2,1,0:T(8,128)(2,1)S(1)} %bitcast.137), kind=kOutput, calls=%fused_computation.36 | convolution fusion | flops 3228565504 | bytes 13631488 | tf_op jit(solution)/shard_map/bj,ejw->ebw/dot_general | solution.py:52
  242.8 8.4 %fusion.10 = f32[2,512,512]{2,1,0:T(8,128)S(1)} fusion(f32[2,512,512]{2,1,0:T(8,128)S(1)} %get-tuple-element.6), kind=kOutput, calls=%fused_computation.17 | convolution fusion | flops 3224895488 | bytes 4194304 | tf_op jit(solution)/shard_map/jb,ebw->ejw/dot_general | solution.py:65
  251.2 8.6 %fusion.12 = f32[2,512,512]{2,1,0:T(8,128)S(1)} fusion(f32[2,512,512]{2,1,0:T(8,128)S(1)} %get-tuple-element.6), kind=kOutput, calls=%fused_computation.19 | convolution fusion | flops 3224895488 | bytes 4194304 | tf_op jit(solution)/shard_map/jb,ebw->ejw/dot_general | solution.py:62
  259.8 8.5 %subtract_bitcast_fusion = f32[1,2,512,512]{2,3,1,0:T(8,128)S(1)} fusion(f32[2,512,512]{2,1,0:T(8,128)S(1)} %fusion.12, f32[2,512,512]{2,1,0:T(8,128)S(1)} %get-tuple-element.5), kind=kOutput, calls=%fused_computation.34 | convolution fusion | flops 3225419776 | bytes 6291456 | tf_op jit(solution)/shard_map/jb,ebw->ejw/dot_general | solution.py:62
  268.3 8.5 %add_bitcast_fusion = f32[1,2,512,512]{2,3,1,0:T(8,128)S(1)} fusion(f32[2,512,512]{2,1,0:T(8,128)S(1)} %fusion.10, f32[2,512,512]{2,1,0:T(8,128)S(1)} %get-tuple-element.5), kind=kOutput, calls=%fused_computation.33 | convolution fusion | flops 3225419776 | bytes 6291456 | tf_op jit(solution)/shard_map/jb,ebw->ejw/dot_general | solution.py:65
  279.1 7.3 %copy.69 = f32[2,2,512,512]{3,1,0,2:T(2,128)} copy(f32[2,2,512,512]{2,3,1,0:T(8,128)} %pad_maximum_fusion) | data formatting | bytes 8388608 | tf_op jit(solution)/shard_map/stack | solution.py:69
  286.4 53.4 %all_to_all.69 = f32[2,2,512,512]{3,1,0,2:T(2,128)S(1)} all-to-all(f32[2,2,512,512]{3,1,0,2:T(2,128)} %copy.69), channel_id=1, replica_groups=mesh['ctx'=8,'tp'=4] {'ctx'}, dimensions={2} | all-to-all | bytes 8388608 | tf_op jit(solution)/shard_map/all_to_all | solution.py:68
  363.8 17.8 %all_to_all.70 = f32[8,64,512]{2,1,0:T(8,128)S(1)} all-to-all(f32[8,64,512]{2,1,0:T(8,128)S(1)} %copy.73), channel_id=1, replica_groups=mesh['ctx'=8,'tp'=4] {'ctx'}, dimensions={0} | all-to-all | bytes 2097152 | tf_op jit(solution)/shard_map/all_to_all | solution.py:78
  (61 shorter events, 60.9 us)
Async XLA Ops:
  6.5 5.9 %copy-start.6 = (f32[3,3,512]{2,1,0:T(4,128)S(1)}, f32[3,3,512]{2,1,0:T(4,128)}, u32[]{:S(2)}) copy-start(f32[3,3,512]{2,1,0:T(4,128)} %param.9) | copy-start | bytes 55300
  6.5 85.9 %all-gather.2.cloned.1.call-start = ((), (), s32[]{:S(2)}) async-start(), calls=%async_computation.6 | async-start | bytes 5242880 | tf_op jit(solution)/shard_map/all_gather | solution.py:84
  7.3 103.7 %all-to-all-start.2 = ((f32[8,64,512]{2,1,0:T(8,128)}), f32[8,64,512]{2,1,0:T(8,128)}, u32[]{:S(2)}, u32[]{:S(2)}) async-start(f32[8,64,512]{2,1,0:T(8,128)} %bitcast.138), calls=%async_computation.2 | async-start | bytes 2097152 | tf_op jit(solution)/shard_map/all_to_all | solution.py:112
  12.4 83.2 %copy-start.8 = (f32[4096]{0:T(1024)S(1)}, f32[4096]{0:T(1024)}, u32[]{:S(2)}) copy-start(f32[4096]{0:T(1024)} %param.7) | copy-start | bytes 49156
  92.4 3.4 copy-start.3
  105.8 2.6 collective-permute-start
  110.9 22.0 %all-to-all-start = ((f32[8,64,512]{2,1,0:T(8,128)}), f32[8,64,512]{2,1,0:T(8,128)}, u32[]{:S(2)}, u32[]{:S(2)}) async-start(f32[8,64,512]{2,1,0:T(8,128)} %bitcast.135), calls=%async_computation | async-start | bytes 2097152 | tf_op jit(solution)/shard_map/all_to_all | solution.py:121
  132.9 3.6 copy-start.2
  145.2 31.0 %all-to-all-start.3 = ((bf16[2,16,64,512]{3,2,0,1:T(8,128)(2,1)}), bf16[2,16,64,512]{3,2,0,1:T(8,128)(2,1)}, u32[]{:S(2)}, u32[]{:S(2)}) async-start(bf16[2,16,64,512]{3,2,0,1:T(8,128)(2,1)} %copy.59), calls=%async_computation.3 | async-start | bytes 4194304 | tf_op jit(solution)/shard_map/all_to_all | solution.py:113
  176.2 35.6 %all-to-all-start.1 = ((bf16[2,16,64,512]{3,2,0,1:T(8,128)(2,1)}), bf16[2,16,64,512]{3,2,0,1:T(8,128)(2,1)}, u32[]{:S(2)}, u32[]{:S(2)}) async-start(bf16[2,16,64,512]{3,2,0,1:T(8,128)(2,1)} %copy.51), calls=%async_computation.1 | async-start | bytes 4194304 | tf_op jit(solution)/shard_map/all_to_all | solution.py:122
  227.8 7.4 %copy-start.4 = (f32[2,512,512]{2,1,0:T(8,128)S(1)}, f32[2,512,512]{2,1,0:T(8,128)}, u32[]{:S(2)}) copy-start(f32[2,512,512]{2,1,0:T(8,128)} %convolution_add_fusion) | copy-start | bytes 6291460
  227.8 7.4 %copy-start.5 = (f32[2,512,512]{2,1,0:T(8,128)S(1)}, f32[2,512,512]{2,1,0:T(8,128)}, u32[]{:S(2)}) copy-start(f32[2,512,512]{2,1,0:T(8,128)} %convolution_subtract_fusion) | copy-start | bytes 6291460
  358.0 3.8 copy-start
  358.0 3.8 copy-start.1
  363.2 18.4 %copy-start.7 = (f32[512]{0:T(512)S(1)}, f32[512]{0:T(512)}, u32[]{:S(2)}) copy-start(f32[512]{0:T(512)} %param.11) | copy-start | bytes 6148
Sparse Core Ops, SparseCore 0:
  8.9 83.4 all-gather.1
where the time goes:
time: 395 us; the launch traced here: 390 us
  matrix products  126 us (32%)
  waiting for transfers between devices  110 us (28%)
  blocking collectives  71.2 us (18%)
  local copies, waits for them, and re-layouts  35.7 us (9%)
  starting transfers between devices  22.4 us (6%)
  between operations  14 us (4%)
  other arithmetic  11.6 us (3%)
    all_gather x1, waiting for transfers between devices, body(): gathered = lax.all_gather(tokens, 'tp', axis=1, tiled=True)  79.9 us
    all_to_all x1, blocking collectives, inverse_transform(): lax.all_to_all(jnp.stack([back_real, back_imag]), 'ctx', split_axis=2, co...  53.4 us
    all_to_all x2, waiting for transfers between devices, body(): lax.all_to_all(values.astype(jnp.bfloat16), 'ctx', split_axis=1, concat_a...  22.4 us
    all_to_all x1, blocking collectives, inverse_transform(): lax.all_to_all(folded.reshape(row_count, width_all), 'ctx', split_axis=0,...  17.8 us
    dot_general x2, matrix products, forward_transform(): jnp.einsum('bj,ejw->ebw', inner_sin, arrived[0], precision=highest)  15.1 us
    dot_general x2, matrix products, forward_transform(): jnp.einsum('bj,ejw->ebw', inner_sin, arrived[1], precision=highest)  14.8 us
    dot_general x2, matrix products, forward_transform(): jnp.einsum('bj,ejw->ebw', inner_cos, arrived[0], precision=highest)  13.8 us
    dot_general x2, matrix products, forward_transform(): jnp.einsum('bj,ejw->ebw', inner_cos, arrived[1], precision=highest)  13.8 us
  transfers between devices with their start and end apart: 6, of which 4 were waited for; matrix products, arithmetic and copies ran while one was open for 16% of the time, Pallas kernels for 0%

commit v1 on v0

--- a/solution.py
+++ b/solution.py
@@ -65,9 +65,10 @@
     back_imag = jnp.einsum("jb,ebw->ejw", inner_sin, spec_real, precision=highest) + jnp.einsum(
         "jb,ebw->ejw", inner_cos, spec_imag, precision=highest
     )
-    arrived = lax.all_to_all(
-        jnp.stack([back_real, back_imag]), "ctx", split_axis=2, concat_axis=1, tiled=True
-    )
+    x = jnp.stack([back_real, back_imag])
+    pieces = jnp.split(x, lax.axis_size("ctx"), axis=2)
+    arrived_2 = lax.all_to_all(jnp.stack(pieces), "ctx", 0, 0)
+    arrived = jnp.concatenate(arrived_2, axis=1)
     turned_real = arrived[0] * twist_cos - arrived[1] * twist_sin
     turned_imag = arrived[0] * twist_sin + arrived[1] * twist_cos
     total_length = 2 * row_count * part_count

time: 395 us -> 365 us (0.924)
  local copies, waits for them, and re-layouts: 35.7 us -> 10.9 us
    slice x3 -> x1, local copies, waits for them, and re-layouts: 9.5 us -> 0.7 us  [inverse_transform(): turned_real = arrived[0] * twist_cos - arrived[1] * twist_sin]
    another operation x1 -> x0, local copies, waits for them, and re-layouts: 7.32 us -> none  [inverse_transform(): jnp.stack([back_real, back_imag])]
    squeeze x2 -> x0, local copies, waits for them, and re-layouts: 7.28 us -> none  [inverse_transform(): turned_real = arrived[0] * twist_cos - arrived[1] * twist_sin]
  transfers between devices with their start and end apart: 6 -> 6, of which waited for: 4 -> 4; matrix products, arithmetic and copies ran while one was open for 16% -> 17% of each run, Pallas kernels for 0% -> 0%
where the time goes in v1:
time: 365 us; the launch traced here: 360 us
  matrix products  123 us (34%)
  waiting for transfers between devices  110 us (30%)
  blocking collectives  70.8 us (19%)
  starting transfers between devices  22.2 us (6%)
  between operations  14 us (4%)
  local copies, waits for them, and re-layouts  10.9 us (3%)
  other arithmetic  9.56 us (3%)
    all_gather x1, waiting for transfers between devices, body(): gathered = lax.all_gather(tokens, 'tp', axis=1, tiled=True)  79.9 us
    all_to_all x1, blocking collectives, inverse_transform(): arrived_2 = lax.all_to_all(jnp.stack(pieces), 'ctx', 0, 0)  53 us
    all_to_all x2, waiting for transfers between devices, body(): lax.all_to_all(values.astype(jnp.bfloat16), 'ctx', split_axis=1, concat_a...  22.4 us
    all_to_all x1, blocking collectives, inverse_transform(): lax.all_to_all(folded.reshape(row_count, width_all), 'ctx', split_axis=0,...  17.8 us
    dot_general x2, matrix products, forward_transform(): jnp.einsum('bj,ejw->ebw', inner_sin, arrived[0], precision=highest)  15.5 us
    dot_general x2, matrix products, forward_transform(): jnp.einsum('bj,ejw->ebw', inner_sin, arrived[1], precision=highest)  14.6 us
    dot_general x2, matrix products, forward_transform(): jnp.einsum('bj,ejw->ebw', inner_cos, arrived[0], precision=highest)  13.8 us
    dot_general x2, matrix products, forward_transform(): jnp.einsum('bj,ejw->ebw', inner_cos, arrived[1], precision=highest)  13.8 us
  transfers between devices with their start and end apart: 6, of which 4 were waited for; matrix products, arithmetic and copies ran while one was open for 17% of the time, Pallas kernels for 0%

profile of v1, /device:TPU:0, one launch (start us, length us, event | category | flops | bytes accessed | tf_op | source)
XLA Modules:
  0.0 360.3 jit_solution(16365154678100561915)
XLA Ops:
  7.3 5.2 %all-to-all-start.2 = ((f32[8,64,512]{2,1,0:T(8,128)}), f32[8,64,512]{2,1,0:T(8,128)}, u32[]{:S(2)}, u32[]{:S(2)}) async-start(f32[8,64,512]{2,1,0:T(8,128)} %bitcast.170), calls=%async_computation.2 | async-start | bytes 2097152 | tf_op jit(solution)/shard_map/all_to_all | solution.py:113
  12.5 79.9 %all-gather.2.cloned.1.call-done = bf16[512,4096]{1,0:T(8,128)(2,1)} async-done(((bf16[512,1024]{1,0:T(8,128)(2,1)}), bf16[512,4096]{1,0:T(8,128)(2,1)}) %all-gather.2.cloned.1.call-update) | async-done | bytes 4194320 | tf_op jit(solution)/shard_map/all_gather | solution.py:85
  95.9 9.9 %fusion.37 = bf16[3,512,512]{2,1,0:T(8,128)(2,1)S(1)} fusion(bf16[3,4096,512]{2,1,0:T(8,128)(2,1)} %param.8, bf16[512,4096]{1,0:T(8,128)(2,1)S(1)} %copy-done.1, f32[4096]{0:T(1024)S(1)} %copy-done.6, f32[512]{0:T(512)S(1)} %add_rsqrt_fusion), kind=kOutput, calls=%fused_computation.67 | convolution fusion | flops 6451625984 | bytes 18368512 | tf_op jit(solution)/shard_map/td,bdc->btc/dot_general | solution.py:89
  110.9 6.3 %all-to-all-start = ((f32[8,64,512]{2,1,0:T(8,128)}), f32[8,64,512]{2,1,0:T(8,128)}, u32[]{:S(2)}, u32[]{:S(2)}) async-start(f32[8,64,512]{2,1,0:T(8,128)} %bitcast.167), calls=%async_computation | async-start | bytes 2097152 | tf_op jit(solution)/shard_map/all_to_all | solution.py:122
  117.4 4.7 %fusion.79 = f32[16,64,512]{2,0,1:T(8,128)} fusion(f32[8,64,512]{2,1,0:T(8,128)} %all-to-all-done.2), kind=kOutput, calls=%fused_computation.106 | convolution fusion | flops 50333440 | bytes 3145728 | tf_op jit(solution)/shard_map/an,njw->ajw/dot_general | solution.py:45
  122.2 4.8 %fusion.81 = f32[16,64,512]{2,0,1:T(8,128)} fusion(f32[8,64,512]{2,1,0:T(8,128)} %all-to-all-done.2), kind=kOutput, calls=%fused_computation.108 | convolution fusion | flops 50333440 | bytes 3145728 | tf_op jit(solution)/shard_map/an,njw->ajw/dot_general | solution.py:44
  127.0 5.7 %all-to-all-done = f32[8,64,512]{2,1,0:T(8,128)} async-done(((f32[8,64,512]{2,1,0:T(8,128)}), f32[8,64,512]{2,1,0:T(8,128)}, u32[]{:S(2)}, u32[]{:S(2)}) %all-to-all-start) | async-done | bytes 1048608 | tf_op jit(solution)/shard_map/all_to_all | solution.py:122
  136.3 5.9 %fusion.51 = (bf16[1,16,64,512]{3,1,2,0:T(8,128)(2,1)S(1)}, bf16[1,16,64,512]{3,1,2,0:T(8,128)(2,1)S(1)}, bf16[1,16,64,512]{3,1,2,0:T(8,128)(2,1)}, bf16[1,16,64,512]{3,1,2,0:T(8,128)(2,1)}) fusion(f32[16,64,512]{2,0,1:T(8,128)S(1)} %copy-done, f32[16,64,512]{2,0,1:T(8,128)} %fusion.81, f32[16,64]{0,1:T(8,128)S(1)} %get-tuple-element.23, ...), kind=kOutput, calls=%fused_computation.75 | convolution fusion | flops 59770624 | bytes 11542528 | tf_op jit(solution)/shard_map/an,njw->ajw/dot_general | solution.py:44
  153.5 22.4 %all-to-all-done.3 = bf16[2,16,64,512]{3,2,0,1:T(8,128)(2,1)} async-done(((bf16[2,16,64,512]{3,2,0,1:T(8,128)(2,1)}), bf16[2,16,64,512]{3,2,0,1:T(8,128)(2,1)}, u32[]{:S(2)}, u32[]{:S(2)}) %all-to-all-start.3) | async-done | bytes 2097184 | tf_op jit(solution)/shard_map/all_to_all | solution.py:114
  175.9 4.6 %all-to-all-start.1 = ((bf16[2,16,64,512]{3,2,0,1:T(8,128)(2,1)}), bf16[2,16,64,512]{3,2,0,1:T(8,128)(2,1)}, u32[]{:S(2)}, u32[]{:S(2)}) async-start(bf16[2,16,64,512]{3,2,0,1:T(8,128)(2,1)} %copy.61), calls=%async_computation.1 | async-start | bytes 4194304 | tf_op jit(solution)/shard_map/all_to_all | solution.py:123
  182.7 6.9 %fusion.68 = f32[2,512,512]{2,1,0:T(8,128)S(1)} fusion(bf16[2,512,512]{2,1,0:T(8,128)(2,1)S(1)} %bitcast.173), kind=kOutput, calls=%fused_computation.95 | convolution fusion | flops 3224895488 | bytes 3145728 | tf_op jit(solution)/shard_map/bj,ejw->ebw/dot_general | solution.py:49
  189.6 6.9 %fusion.64 = f32[2,512,512]{2,1,0:T(8,128)S(1)} fusion(bf16[2,512,512]{2,1,0:T(8,128)(2,1)S(1)} %bitcast.171), kind=kOutput, calls=%fused_computation.91 | convolution fusion | flops 3224895488 | bytes 3145728 | tf_op jit(solution)/shard_map/bj,ejw->ebw/dot_general | solution.py:52
  196.5 7.4 %convolution_add_fusion = f32[2,512,512]{2,1,0:T(8,128)} fusion(f32[2,512,512]{2,1,0:T(8,128)S(1)} %fusion.68, bf16[2,512,512]{2,1,0:T(8,128)(2,1)S(1)} %bitcast.172), kind=kOutput, calls=%fused_computation.61 | convolution fusion | flops 3225419776 | bytes 5242880 | tf_op jit(solution)/shard_map/bj,ejw->ebw/dot_general | solution.py:49
  203.9 7.8 %convolution_subtract_fusion = f32[2,512,512]{2,1,0:T(8,128)} fusion(f32[2,512,512]{2,1,0:T(8,128)S(1)} %fusion.64, bf16[2,512,512]{2,1,0:T(8,128)(2,1)S(1)} %bitcast.174), kind=kOutput, calls=%fused_computation.59 | convolution fusion | flops 3225419776 | bytes 5242880 | tf_op jit(solution)/shard_map/bj,ejw->ebw/dot_general | solution.py:52
  213.9 6.9 %fusion.66 = f32[2,512,512]{2,1,0:T(8,128)S(1)} fusion(bf16[2,512,512]{2,1,0:T(8,128)(2,1)S(1)} %bitcast.175), kind=kOutput, calls=%fused_computation.93 | convolution fusion | flops 3224895488 | bytes 3145728 | tf_op jit(solution)/shard_map/bj,ejw->ebw/dot_general | solution.py:52
  220.9 6.9 %fusion.70 = f32[2,512,512]{2,1,0:T(8,128)S(1)} fusion(bf16[2,512,512]{2,1,0:T(8,128)(2,1)S(1)} %bitcast.168), kind=kOutput, calls=%fused_computation.97 | convolution fusion | flops 3224895488 | bytes 3145728 | tf_op jit(solution)/shard_map/bj,ejw->ebw/dot_general | solution.py:49
  227.8 7.2 %convolution_add_fusion.1 = f32[2,512,512]{2,1,0:T(8,128)S(1)} fusion(f32[2,512,512]{2,1,0:T(8,128)S(1)} %fusion.70, bf16[2,512,512]{2,1,0:T(8,128)(2,1)S(1)} %bitcast.176), kind=kOutput, calls=%fused_computation.62 | convolution fusion | flops 3225419776 | bytes 5242880 | tf_op jit(solution)/shard_map/bj,ejw->ebw/dot_general | solution.py:49
  235.0 7.7 %multiply_subtract_fusion = (f32[2,512,512]{2,1,0:T(8,128)S(1)}, f32[2,512,512]{2,1,0:T(8,128)S(1)}) fusion(f32[2,512,512]{2,1,0:T(8,128)S(1)} %copy-done.3, f32[2,512,512]{2,1,0:T(8,128)S(1)} %convolution_add_fusion.1, f32[2,512,512]{2,1,0:T(8,128)S(1)} %copy-done.2, f32[2,512,512]{2,1,0:T(8,128)S(1)} %fusion.66, bf16[2,512,512]{2,1,0:T(8,128)(2,1)S(1)} %bitcast.169), kind=kOutput, calls=%fused_computation.49 | convolution fusion | flops 3228565504 | bytes 13631488 | tf_op jit(solution)/shard_map/bj,ejw->ebw/dot_general | solution.py:52
  242.7 7.3 %fusion.10 = f32[2,512,512]{1,2,0:T(8,128)S(1)} fusion(f32[2,512,512]{2,1,0:T(8,128)S(1)} %get-tuple-element.6), kind=kOutput, calls=%fused_computation.30 | convolution fusion | flops 3224895488 | bytes 4194304 | tf_op jit(solution)/shard_map/jb,ebw->ejw/dot_general | solution.py:65
  250.1 7.8 %fusion.12 = f32[2,512,512]{1,2,0:T(8,128)S(1)} fusion(f32[2,512,512]{2,1,0:T(8,128)S(1)} %get-tuple-element.6), kind=kOutput, calls=%fused_computation.32 | convolution fusion | flops 3224895488 | bytes 4194304 | tf_op jit(solution)/shard_map/jb,ebw->ejw/dot_general | solution.py:62
  257.9 7.4 %add_bitcast_fusion = f32[1,2,512,512]{3,2,1,0:T(8,128)S(1)} fusion(f32[2,512,512]{1,2,0:T(8,128)S(1)} %fusion.10, f32[2,512,512]{2,1,0:T(8,128)S(1)} %get-tuple-element.5), kind=kOutput, calls=%fused_computation.46 | convolution fusion | flops 3225419776 | bytes 6291456 | tf_op jit(solution)/shard_map/jb,ebw->ejw/dot_general | solution.py:65
  265.3 7.5 %subtract_bitcast_fusion = f32[1,2,512,512]{3,2,1,0:T(8,128)S(1)} fusion(f32[2,512,512]{1,2,0:T(8,128)S(1)} %fusion.12, f32[2,512,512]{2,1,0:T(8,128)S(1)} %get-tuple-element.5), kind=kOutput, calls=%fused_computation.47 | convolution fusion | flops 3225419776 | bytes 6291456 | tf_op jit(solution)/shard_map/jb,ebw->ejw/dot_general | solution.py:62
  273.2 53.0 %all_to_all.59 = f32[8,2,2,64,512]{4,3,2,1,0:T(8,128)S(1)} all-to-all(f32[8,2,2,64,512]{4,3,2,1,0:T(8,128)S(1)} %fusion.109), channel_id=1, replica_groups=mesh['ctx'=8,'tp'=4] {'ctx'}, dimensions={0} | all-to-all | bytes 8388608 | tf_op jit(solution)/shard_map/all_to_all | solution.py:70
  334.2 17.8 %all_to_all.60 = f32[8,64,512]{2,1,0:T(8,128)S(1)} all-to-all(f32[8,64,512]{2,1,0:T(8,128)S(1)} %copy.85), channel_id=1, replica_groups=mesh['ctx'=8,'tp'=4] {'ctx'}, dimensions={0} | all-to-all | bytes 2097152 | tf_op jit(solution)/shard_map/all_to_all | solution.py:79
  (58 shorter events, 38.3 us)
Async XLA Ops:
  6.5 5.9 %copy-start.4 = (f32[3,3,512]{2,1,0:T(4,128)S(1)}, f32[3,3,512]{2,1,0:T(4,128)}, u32[]{:S(2)}) copy-start(f32[3,3,512]{2,1,0:T(4,128)} %param.9) | copy-start | bytes 55300
  6.5 85.9 %all-gather.2.cloned.1.call-start = ((), (), s32[]{:S(2)}) async-start(), calls=%async_computation.6 | async-start | bytes 5242880 | tf_op jit(solution)/shard_map/all_gather | solution.py:85
  7.3 103.7 %all-to-all-start.2 = ((f32[8,64,512]{2,1,0:T(8,128)}), f32[8,64,512]{2,1,0:T(8,128)}, u32[]{:S(2)}, u32[]{:S(2)}) async-start(f32[8,64,512]{2,1,0:T(8,128)} %bitcast.170), calls=%async_computation.2 | async-start | bytes 2097152 | tf_op jit(solution)/shard_map/all_to_all | solution.py:113
  12.4 83.2 %copy-start.6 = (f32[4096]{0:T(1024)S(1)}, f32[4096]{0:T(1024)}, u32[]{:S(2)}) copy-start(f32[4096]{0:T(1024)} %param.7) | copy-start | bytes 49156
  92.4 3.4 copy-start.1
  105.8 2.6 collective-permute-start
  110.9 21.7 %all-to-all-start = ((f32[8,64,512]{2,1,0:T(8,128)}), f32[8,64,512]{2,1,0:T(8,128)}, u32[]{:S(2)}, u32[]{:S(2)}) async-start(f32[8,64,512]{2,1,0:T(8,128)} %bitcast.167), calls=%async_computation | async-start | bytes 2097152 | tf_op jit(solution)/shard_map/all_to_all | solution.py:122
  132.7 3.6 copy-start
  144.9 31.0 %all-to-all-start.3 = ((bf16[2,16,64,512]{3,2,0,1:T(8,128)(2,1)}), bf16[2,16,64,512]{3,2,0,1:T(8,128)(2,1)}, u32[]{:S(2)}, u32[]{:S(2)}) async-start(bf16[2,16,64,512]{3,2,0,1:T(8,128)(2,1)} %copy.69), calls=%async_computation.3 | async-start | bytes 4194304 | tf_op jit(solution)/shard_map/all_to_all | solution.py:114
  175.9 35.9 %all-to-all-start.1 = ((bf16[2,16,64,512]{3,2,0,1:T(8,128)(2,1)}), bf16[2,16,64,512]{3,2,0,1:T(8,128)(2,1)}, u32[]{:S(2)}, u32[]{:S(2)}) async-start(bf16[2,16,64,512]{3,2,0,1:T(8,128)(2,1)} %copy.61), calls=%async_computation.1 | async-start | bytes 4194304 | tf_op jit(solution)/shard_map/all_to_all | solution.py:123
  227.8 7.2 %copy-start.2 = (f32[2,512,512]{2,1,0:T(8,128)S(1)}, f32[2,512,512]{2,1,0:T(8,128)}, u32[]{:S(2)}) copy-start(f32[2,512,512]{2,1,0:T(8,128)} %convolution_add_fusion) | copy-start | bytes 6291460
  227.8 7.2 %copy-start.3 = (f32[2,512,512]{2,1,0:T(8,128)S(1)}, f32[2,512,512]{2,1,0:T(8,128)}, u32[]{:S(2)}) copy-start(f32[2,512,512]{2,1,0:T(8,128)} %convolution_subtract_fusion) | copy-start | bytes 6291460
  333.6 18.4 %copy-start.5 = (f32[512]{0:T(512)S(1)}, f32[512]{0:T(512)}, u32[]{:S(2)}) copy-start(f32[512]{0:T(512)} %param.11) | copy-start | bytes 6148
Sparse Core Ops, SparseCore 0:
  8.9 83.4 all-gather.1
